TPU v7x, 32 devices: a whole 2x2x4 slice. The times are simulated.
32 devices in a mesh: grp: 2 (over y), gx: 4 (over z), gy: 2 (over x), gz: 2 (over core).
Axes of the slice: x: 2, y: 2, z: 4, core: 2. Of those that a mesh axis runs over, the one named last changes fastest.
Arguments:
- atom_feats: bfloat16 [8, 2, 128, 2304], P(('grp', 'gx'), 'gy'), parts along dimension 0, may hold values from -6 to 6
- atom_pos: float32 [8, 2, 3, 128], P(('grp', 'gx'), 'gy'), parts along dimension 0, may hold values from 0 to 1
- species: int32 [8, 2, 128], P(('grp', 'gx'), 'gy'), parts along dimension 0, may hold values from 0 to 4
- species_gain: float32 [5, 256], replicated, may hold values from 0.5 to 2
- probe_pos: float32 [3, 8192], P(None, ('grp', 'gx', 'gy', 'gz')), parts along dimension 1, may hold values from 0 to 1
- pair_slot: int32 [64, 4], P(('grp', 'gx', 'gy', 'gz')), parts along dimension 0, may hold values from 0 to 8
- pair_count: int32 [64], P(('grp', 'gx', 'gy', 'gz')), parts along dimension 0, may hold values from 1 to 4, as said below
- w_rad: float32 [3, 8, 256], replicated, may hold values from -0.5 to 0.5
- w_one: bfloat16 [256, 256], replicated, may hold values from -0.375 to 0.375
- w_two: float32 [256], replicated, may hold values from -0.375 to 0.375
- target: float32 [8192], P(('grp', 'gx', 'gy', 'gz')), parts along dimension 0, may hold values from -96 to 96
Outputs:
- density: float32 [8192], P(('grp', 'gx', 'gy', 'gz')), parts along dimension 0
- grad_one: float32 [512, 256], P('grp'), parts along dimension 0
- grad_two: float32 [512], P('grp'), parts along dimension 0
There are 2 independent parts, one for each index of `grp`. A program takes and returns all parts, laid end to end along the dimension named above; an argument that names none is the same for every part. Nothing has to cross between parts.
Inputs may be any that keep to these rules, and one draw needn't show every extreme that they name: `pair_count`: each probe block uses between 1 and 4 entries; some block uses all 4.
All inputs are finite; a program needn't handle non-finite values.
Results may differ from a plain program's by a relative error of at most 0.0061.
Values may be sent and summed in bfloat16 or wider, within the bound.
A program may use at most 64 MiB of HBM per device.

v0:
```python
import functools
import math

import jax
import jax.numpy as jnp
from jax import lax
from jax.experimental import pallas as pl
from jax.experimental.pallas import tpu as pltpu
from jax.sharding import PartitionSpec as P

MESH = pl.DeviceIdType.MESH
PBLK = 128
side_x = 8.0
side_y = 8.0
side_z = 25.0
cutoff = 4.0
sqrt_three = 1.7320508075688772
CHUNKS = ((1, 4), (4, 7), (7, 9), (0, 1))
DEGREE = (1, 2, 2, 0)
Y_FIRST = (2, 3)
ROWS = 16


def kernel(
    nx,
    ny,
    feats,
    pos,
    spec,
    gain,
    probe,
    slot,
    count,
    w_rad,
    w_one,
    w_two,
    target,
    density_out,
    one_out,
    two_out,
    tab0,
    tab1,
    tab2,
    tab3,
    posb,
    edges,
    pmap,
    msg,
    ici_send,
    ici_recv,
    sib_send,
    sib_recv,
    pos_send,
    pos_recv,
    *reduce_refs,
):
    tabs = (tab0, tab1, tab2, tab3)
    nentry = slot.shape[1]
    nblocks = slot.shape[0]
    nrad = w_rad.shape[1]
    natoms, chans = tab0.shape[2], tab0.shape[3]
    dys = (0, 1) if ny == 2 else (0, 1, -1)
    dxs = (0, 1, -1)
    nyc = len(dys)
    ncol = 3 * nyc
    gx, gy, gz = lax.axis_index("gx"), lax.axis_index("gy"), lax.axis_index("gz")
    sibling = {"gz": 1 - gz}

    def at(dx, dy):
        return {"gx": lax.rem(gx + dx + nx, nx), "gy": lax.rem(gy + dy + ny, ny)}

    remote = [(xi, yi) for xi in range(3) for yi in range(nyc) if (xi, yi) != (0, 0)]
    chips = nx * ny
    me = gx * ny + gy
    offsets = range(1, chips)

    def peer(offset):
        other = lax.rem(me + offset, chips)
        return {"gx": other // ny, "gy": lax.rem(other, ny)}

    barrier = pltpu.get_barrier_semaphore()
    if reduce_refs:
        greeted = [peer(offset) for offset in offsets]
    else:
        greeted = [at(-dxs[xi], -dys[yi]) for xi, yi in remote]
    for device in greeted:
        pl.semaphore_signal(barrier, inc=1, device_id=device, device_id_type=MESH)
    pl.semaphore_signal(barrier, inc=1, device_id=sibling, device_id_type=MESH)

    nspec = gain.shape[0]
    onehot = (lax.broadcasted_iota(jnp.int32, (nspec, natoms), 0) == spec[...]).astype(jnp.float32)
    gains = lax.dot_general(
        onehot,
        gain[...],
        (((0,), (0,)), ((), ())),
        precision=lax.Precision.HIGHEST,
        preferred_element_type=jnp.float32,
    )
    for (low, high), tab in zip(CHUNKS, tabs):
        for k in range(low, high):
            raw = feats[:, k * chans : (k + 1) * chans].astype(jnp.float32)
            tab[0, k - low] = (raw * gains).astype(jnp.bfloat16)
    posb[0] = pos[...]
    for block in range(nblocks):
        for axis in range(3):
            row = probe[axis : axis + 1, block * PBLK : (block + 1) * PBLK]
            pmap[block, axis] = jnp.transpose(jnp.broadcast_to(row, (PBLK, PBLK)))
    msg[...] = jnp.zeros_like(msg)
    pl.semaphore_wait(barrier, len(greeted) + 1)

    half = natoms // 2
    rows = pl.ds(pl.multiple_of(gz * half, half), half)

    def ici(c, xi, yi):
        tab = tabs[c]
        if yi == 0:
            source, dev = 0, at(-dxs[xi], 0)
        elif xi == 0:
            source, dev = 0, at(0, -dys[yi])
        elif c in Y_FIRST:
            source, dev = yi, at(-dxs[xi], 0)
        else:
            source, dev = xi * nyc, at(0, -dys[yi])
        col = xi * nyc + yi
        return pltpu.make_async_remote_copy(
            src_ref=tab.at[source, :, rows, :],
            dst_ref=tab.at[col, :, rows, :],
            send_sem=ici_send.at[c, col],
            recv_sem=ici_recv.at[c, col],
            device_id=dev,
            device_id_type=MESH,
        )

    def sib(c, xi, yi):
        tab = tabs[c]
        col = xi * nyc + yi
        return pltpu.make_async_remote_copy(
            src_ref=tab.at[col, :, rows, :],
            dst_ref=tab.at[col, :, rows, :],
            send_sem=sib_send.at[c, col],
            recv_sem=sib_recv.at[c, col],
            device_id=sibling,
            device_id_type=MESH,
        )

    def pos_copy(xi, yi):
        col = xi * nyc + yi
        return pltpu.make_async_remote_copy(
            src_ref=pos,
            dst_ref=posb.at[col],
            send_sem=pos_send.at[col],
            recv_sem=pos_recv.at[col],
            device_id=at(-dxs[xi], -dys[yi]),
            device_id_type=MESH,
        )

    along_x = [(xi, yi) for xi, yi in remote if yi == 0]
    along_y = [(xi, yi) for xi, yi in remote if xi == 0]
    second = [(xi, yi) for xi, yi in remote if xi != 0 and yi != 0]
    for xi, yi in remote:
        pos_copy(xi, yi).start()
    chunk_ids = range(len(CHUNKS))
    for c in chunk_ids:
        for xi, yi in along_x:
            ici(c, xi, yi).start()
    for c in sorted(chunk_ids, key=lambda c: c not in Y_FIRST):
        for xi, yi in along_y:
            ici(c, xi, yi).start()

    def pass_x(c):
        for xi, yi in along_x:
            ici(c, xi, yi).wait_recv()
            if c not in Y_FIRST:
                for sx, sy in second:
                    if sx == xi:
                        ici(c, sx, sy).start()
            sib(c, xi, yi).start()

    def pass_y(c):
        for xi, yi in along_y:
            ici(c, xi, yi).wait_recv()
            if c in Y_FIRST:
                for sx, sy in second:
                    if sy == yi:
                        ici(c, sx, sy).start()
            sib(c, xi, yi).start()

    def pass_second(c):
        for xi, yi in second:
            ici(c, xi, yi).wait_recv()
            sib(c, xi, yi).start()

    def column_of(block, entry):
        s = slot[block, entry]
        xi = lax.rem(s // 3 + 2, 3)
        yi = lax.rem(s % 3 + 1, 2) if ny == 2 else lax.rem(s % 3 + 2, 3)
        return xi * nyc + yi

    gamma = 0.5 * (nrad / cutoff) ** 2
    rc2 = cutoff * cutoff

    def edge_unit(unit, _):
        block = unit // nentry
        entry = unit % nentry
        s = slot[block, entry]
        shift_x = (s // 3 - 1).astype(jnp.float32)
        shift_y = (s % 3 - 1).astype(jnp.float32)
        used = (entry < count[block]).astype(jnp.float32)
        atoms = posb[column_of(block, entry)]
        ax = atoms[0] + shift_x
        ay = atoms[1] + shift_y
        az = atoms[2]

        def strip(i, _):
            at_row = pl.multiple_of(i * ROWS, ROWS)
            dist_x = (ax - pmap[block, 0, pl.ds(at_row, ROWS), :]) * side_x
            dist_y = (ay - pmap[block, 1, pl.ds(at_row, ROWS), :]) * side_y
            dist_z = (az - pmap[block, 2, pl.ds(at_row, ROWS), :]) * side_z
            radius2 = dist_x * dist_x + dist_y * dist_y + dist_z * dist_z
            smooth = jnp.where(radius2 < rc2, (1.0 - radius2 / rc2) ** 2, 0.0) * used
            radius = jnp.sqrt(radius2)
            hx, hy, hz = dist_x / cutoff, dist_y / cutoff, dist_z / cutoff
            harmonics = (
                None,
                hx,
                hy,
                hz,
                sqrt_three * hx * hy,
                sqrt_three * hy * hz,
                (3.0 * dist_z * dist_z - radius2) * (0.5 / rc2),
                sqrt_three * hx * hz,
                (0.5 * sqrt_three) * (hx * hx - hy * hy),
            )
            for b in range(nrad):
                offset = radius - cutoff * b / (nrad - 1)
                basis = jnp.exp(-gamma * (offset * offset)) * smooth
                for k in range(9):
                    value = basis if k == 0 else basis * harmonics[k]
                    edges[block, k, entry, pl.ds(b * PBLK + at_row, ROWS), :] = value.astype(
                        jnp.bfloat16
                    )
            return 0

        lax.fori_loop(0, PBLK // ROWS, strip, 0)
        return 0

    def matmul(c):
        low, high = CHUNKS[c]
        for xi, yi in remote:
            sib(c, xi, yi).wait_recv()

        def one_block(block, _):
            weights = []
            cols = [column_of(block, entry) for entry in range(nentry)]
            for k in range(high - low):
                for entry in range(nentry):
                    weights.append(tabs[c][cols[entry], k])
            weights = jnp.concatenate(weights, axis=0)
            lhs = jnp.concatenate(
                [
                    edges[block, k, entry]
                    for k in range(low, high)
                    for entry in range(nentry)
                ],
                axis=1,
            )
            part = jnp.dot(lhs, weights, preferred_element_type=jnp.float32)
            total = msg[block]
            for b in range(nrad):
                total = total + part[b * PBLK : (b + 1) * PBLK] * w_rad[DEGREE[c], b : b + 1, :]
            msg[block] = total
            return 0

        lax.fori_loop(0, nblocks, one_block, 0)

    for xi, yi in remote:
        pos_copy(xi, yi).wait_recv()
    units = nblocks * nentry
    lax.fori_loop(0, units // 8, edge_unit, 0)
    pass_y(2)
    pass_y(3)
    lax.fori_loop(units // 8, 4 * units // 8, edge_unit, 0)
    pass_x(0)
    pass_y(0)
    lax.fori_loop(4 * units // 8, 6 * units // 8, edge_unit, 0)
    pass_y(1)
    lax.fori_loop(6 * units // 8, units, edge_unit, 0)
    pass_x(1)
    pass_second(0)
    pass_x(2)
    matmul(0)
    pass_x(3)
    pass_second(1)
    pass_second(2)
    matmul(1)
    pass_second(3)
    matmul(2)
    matmul(3)

    message_bf = msg[...].reshape(nblocks * PBLK, chans).astype(jnp.bfloat16)
    pre = jnp.dot(message_bf, w_one[...], preferred_element_type=jnp.float32)
    sigm = jax.nn.sigmoid(pre)
    act = pre * sigm
    dens = jnp.sum(act * w_two[...], axis=1, keepdims=True)
    goals = []
    for block in range(nblocks):
        column = dens[block * PBLK : (block + 1) * PBLK]
        flat = jnp.transpose(jnp.broadcast_to(column, (PBLK, PBLK)))
        density_out[block : block + 1, :] = flat[0:1]
        goal = jnp.transpose(jnp.broadcast_to(target[block : block + 1, :], (PBLK, PBLK)))
        goals.append(goal[:, 0:1])
    goals = jnp.concatenate(goals, axis=0)
    total_probes = nblocks * PBLK * nx * ny * 2
    grad_out = (dens - goals) * jnp.float32(1.0 / math.sqrt(total_probes))
    dpre = (grad_out * w_two[...] * sigm * (1.0 + pre * (1.0 - sigm))).astype(jnp.bfloat16)
    local_one = lax.dot_general(
        message_bf, dpre, (((0,), (0,)), ((), ())), preferred_element_type=jnp.float32
    )
    local_two = jnp.sum(grad_out * act, axis=0, keepdims=True)
    if not reduce_refs:
        one_out[...] = local_one
        two_out[...] = local_two
    else:
        (
            part,
            two_part,
            pair_in,
            two_pair_in,
            shares,
            two_share,
            shares_in,
            two_in,
            gathered,
            pair_send,
            pair_recv,
            share_send,
            share_recv,
            two_send,
            two_recv,
            full_send,
            full_recv,
        ) = reduce_refs
        upper = chans // 2
        span = upper // chips
        part[...] = local_one.reshape(2, upper, chans)
        two_part[...] = local_two

        def to_sibling(index, source, dest):
            return pltpu.make_async_remote_copy(
                src_ref=source,
                dst_ref=dest,
                send_sem=pair_send.at[index],
                recv_sem=pair_recv.at[index],
                device_id=sibling,
                device_id_type=MESH,
            )

        def to_peer(offset, source, dest, send, recv):
            return pltpu.make_async_remote_copy(
                src_ref=source,
                dst_ref=dest,
                send_sem=send.at[offset],
                recv_sem=recv.at[offset],
                device_id=peer(offset),
                device_id_type=MESH,
            )

        swaps = [to_sibling(0, part.at[1 - gz], pair_in), to_sibling(1, two_part, two_pair_in)]
        for copy in swaps:
            copy.start()
        for copy in swaps:
            copy.wait_recv()
        chip_sum = part[gz] + pair_in[...]
        shares[...] = chip_sum.reshape(chips, span, chans).astype(jnp.bfloat16)
        two_sum = two_part[...] + two_pair_in[...]
        two_share[...] = two_sum
        two_in[me] = two_sum
        scattered = []
        for offset in offsets:
            target_chip = lax.rem(me + offset, chips)
            scattered.append(
                to_peer(offset, shares.at[target_chip], shares_in.at[offset], share_send, share_recv)
            )
        twos = [to_peer(offset, two_share, two_in.at[me], two_send, two_recv) for offset in offsets]
        for copy in scattered + twos:
            copy.start()
        total = shares[me].astype(jnp.float32)
        for offset, copy in zip(offsets, scattered):
            copy.wait_recv()
            total = total + shares_in[offset].astype(jnp.float32)
        gathered[gz, me] = total.astype(jnp.bfloat16)
        spread = [
            to_peer(offset, gathered.at[gz, me], gathered.at[gz, me], full_send, full_recv)
            for offset in offsets
        ]
        for copy in spread:
            copy.start()
        for copy in twos:
            copy.wait_recv()
        two_out[...] = jnp.sum(two_in[...], axis=0)
        for copy in spread:
            copy.wait_recv()
        swap_back = to_sibling(2, gathered.at[gz], gathered.at[gz])
        swap_back.start()
        swap_back.wait_recv()
        one_out[...] = gathered[...].reshape(chans, chans)
        for copy in swaps + scattered + twos + spread + [swap_back]:
            copy.wait_send()

    for xi, yi in remote:
        pos_copy(xi, yi).wait_send()
        for c in range(len(CHUNKS)):
            ici(c, xi, yi).wait_send()
            sib(c, xi, yi).wait_send()


def on_device(
    nx,
    ny,
    atom_feats,
    atom_pos,
    species,
    species_gain,
    probe_pos,
    pair_slot,
    pair_count,
    w_rad,
    w_one,
    w_two,
    target,
):
    natoms = atom_feats.shape[2]
    chans = w_one.shape[0]
    nblocks = pair_slot.shape[0]
    nentry = pair_slot.shape[1]
    nrad = w_rad.shape[1]
    ncol = 6 if ny == 2 else 9
    vmem = pl.BlockSpec(memory_space=pltpu.VMEM)
    smem = pl.BlockSpec(memory_space=pltpu.SMEM)
    nchunk = len(CHUNKS)
    chips = nx * ny
    fused = (chans // 2) % (16 * chips) == 0
    reduce_scratch = []
    if fused:
        span = chans // 2 // chips
        reduce_scratch = [
            pltpu.VMEM((2, chans // 2, chans), jnp.float32),
            pltpu.VMEM((1, chans), jnp.float32),
            pltpu.VMEM((chans // 2, chans), jnp.float32),
            pltpu.VMEM((1, chans), jnp.float32),
            pltpu.VMEM((chips, span, chans), jnp.bfloat16),
            pltpu.VMEM((1, chans), jnp.float32),
            pltpu.VMEM((chips, span, chans), jnp.bfloat16),
            pltpu.VMEM((chips, 1, chans), jnp.float32),
            pltpu.VMEM((2, chips, span, chans), jnp.bfloat16),
            pltpu.SemaphoreType.DMA((3,)),
            pltpu.SemaphoreType.DMA((3,)),
            *[pltpu.SemaphoreType.DMA((chips,)) for _ in range(6)],
        ]
    density, one, two = pl.pallas_call(
        functools.partial(kernel, nx, ny),
        out_shape=(
            jax.ShapeDtypeStruct((nblocks, PBLK), jnp.float32),
            jax.ShapeDtypeStruct((chans, chans), jnp.bfloat16 if fused else jnp.float32),
            jax.ShapeDtypeStruct((1, chans), jnp.float32),
        ),
        in_specs=[vmem, vmem, vmem, vmem, vmem, smem, smem, vmem, vmem, vmem, vmem],
        out_specs=(vmem, vmem, vmem),
        scratch_shapes=[
            *[
                pltpu.VMEM((ncol, high - low, natoms, chans), jnp.bfloat16)
                for low, high in CHUNKS
            ],
            pltpu.VMEM((ncol, 3, 1, natoms), jnp.float32),
            pltpu.VMEM((nblocks, 9, nentry, nrad * PBLK, natoms), jnp.bfloat16),
            pltpu.VMEM((nblocks, 3, PBLK, PBLK), jnp.float32),
            pltpu.VMEM((nblocks, PBLK, chans), jnp.float32),
            pltpu.SemaphoreType.DMA((nchunk, ncol)),
            pltpu.SemaphoreType.DMA((nchunk, ncol)),
            pltpu.SemaphoreType.DMA((nchunk, ncol)),
            pltpu.SemaphoreType.DMA((nchunk, ncol)),
            pltpu.SemaphoreType.DMA((ncol,)),
            pltpu.SemaphoreType.DMA((ncol,)),
            *reduce_scratch,
        ],
        compiler_params=pltpu.CompilerParams(
            collective_id=0, has_side_effects=True, vmem_limit_bytes=60 * 1024 * 1024
        ),
    )(
        atom_feats.reshape(natoms, -1),
        atom_pos.reshape(3, 1, natoms),
        species.reshape(1, natoms),
        species_gain,
        probe_pos,
        pair_slot,
        pair_count,
        w_rad,
        w_one,
        w_two.reshape(1, chans),
        target.reshape(nblocks, PBLK),
    )
    two = two.reshape(chans)
    if fused:
        one = one.astype(jnp.float32)
    else:
        one, two = lax.psum((one, two), ("gx", "gy", "gz"))
    return density.reshape(-1), one, two


def solution(mesh):
    return jax.shard_map(
        functools.partial(on_device, mesh.shape["gx"], mesh.shape["gy"]),
        mesh=mesh,
        in_specs=(
            P(("grp", "gx"), "gy", None, None),
            P(("grp", "gx"), "gy", None, None),
            P(("grp", "gx"), "gy", None),
            P(),
            P(None, ("grp", "gx", "gy", "gz")),
            P(("grp", "gx", "gy", "gz"), None),
            P(("grp", "gx", "gy", "gz")),
            P(),
            P(),
            P(),
            P(("grp", "gx", "gy", "gz")),
        ),
        out_specs=(P(("grp", "gx", "gy", "gz")), P("grp", None), P("grp")),
        check_vma=False,
    )
```

profile of v0, /device:TPU:0, one launch (start us, length us, event | category | flops | bytes accessed | tf_op | source)
XLA Modules:
  0.0 46.1 jit_solution(868812632267066900)
XLA Ops:
  0.6 42.6 %shard_map.130 = (f32[2,128]{1,0:T(2,128)}, bf16[256,256]{1,0:T(8,128)(2,1)}, f32[1,256]{1,0:T(1,128)}) custom-call(bf16[128,2304]{1,0:T(8,128)(2,1)} %bitcast.7, f32[3,1,128]{2,1,0:T(1,128)} %bitcast.8, s32[1,128]{1,0:T(1,128)} %bitcast.13, f32[5,256]{1,0:T(8,128)} %gain.1, f32[3,256]{1,0:T(4,128)} %probe.1, s32[2,4]{1,0:T(2,128)} %slot.1, s32[2]{0:T(128)} %count.1, ...), custom_call_target="tpu_custom_call" | custom-call | tf_op jit(solution)/shard_map/pallas_call | solution.py:460
  43.2 0.0 copy-start.1
  43.3 1.6 %convert_element_type.3 = f32[256,256]{1,0:T(8,128)} convert(bf16[256,256]{1,0:T(8,128)(2,1)} %get-tuple-element.7) | non-fusion elementwise | flops 65536 | bytes 393216 | tf_op jit(solution)/shard_map/convert_element_type | solution.py:504
  44.9 0.0 copy-done.1
  44.9 0.0 copy-start
  44.9 0.6 %copy.16 = f32[256]{0:T(256)} copy(f32[256]{0:T(256)S(1)} %bitcast.12) | data formatting | bytes 2048
  45.5 0.1 copy-done
  45.6 0.6 %copy.17 = f32[256]{0:T(256)} copy(f32[256]{0:T(256)S(1)} %bitcast.11) | data formatting | bytes 2048
Async XLA Ops:
  43.2 1.6 %copy-start.1 = (f32[2,128]{1,0:T(2,128)S(1)}, f32[2,128]{1,0:T(2,128)}, u32[]{:S(2)}) copy-start(f32[2,128]{1,0:T(2,128)} %get-tuple-element.6) | copy-start | bytes 3076
  44.9 0.7 %copy-start = (f32[1,256]{1,0:T(1,128)S(1)}, f32[1,256]{1,0:T(1,128)}, u32[]{:S(2)}) copy-start(f32[1,256]{1,0:T(1,128)} %get-tuple-element.8) | copy-start | bytes 3076
where the time goes:
time: 46.3 us; the launch traced here: 46.1 us
  Pallas kernels  42.6 us (92%)
  other arithmetic  1.63 us (4%)
  local copies, waits for them, and re-layouts  1.23 us (3%)
  between operations  0.65 us (1%)
    pallas_call x1, Pallas kernels, on_device(): pl.pallas_call(functools.partial(kernel, nx, ny), out_shape=(jax.ShapeDty...  42.6 us
    convert_element_type x1, other arithmetic, on_device(): one = one.astype(jnp.float32)  1.63 us
    unnamed x6, local copies, waits for them, and re-layouts  1.23 us

commit v1 on v0

--- a/solution.py
+++ b/solution.py
@@ -15,15 +15,31 @@
 side_z = 25.0
 cutoff = 4.0
 sqrt_three = 1.7320508075688772
-CHUNKS = ((1, 4), (4, 7), (7, 9), (0, 1))
-DEGREE = (1, 2, 2, 0)
-Y_FIRST = (2, 3)
+CHUNKS = ((1, 2), (2, 4), (4, 6), (6, 8), (8, 9), (0, 1))
+DEGREE = (1, 1, 2, 2, 2, 0)
+Y_FIRST = (3,)
+X_ORDER = (0, 1, 2, 4, 5, 3)
+FUSED_CHIPS = 8
 ROWS = 16
 
 
 def kernel(
     nx,
     ny,
+    feats_in,
+    pos_in,
+    spec_in,
+    gain_in,
+    probe_in,
+    slot_in,
+    count_in,
+    w_rad_in,
+    w_one_in,
+    w_two_in,
+    target_in,
+    density_out,
+    one_out,
+    two_out,
     feats,
     pos,
     spec,
@@ -35,13 +51,13 @@
     w_one,
     w_two,
     target,
-    density_out,
-    one_out,
-    two_out,
+    load_sem,
     tab0,
     tab1,
     tab2,
     tab3,
+    tab4,
+    tab5,
     posb,
     edges,
     pmap,
@@ -54,7 +70,7 @@
     pos_recv,
     *reduce_refs,
 ):
-    tabs = (tab0, tab1, tab2, tab3)
+    tabs = (tab0, tab1, tab2, tab3, tab4, tab5)
     nentry = slot.shape[1]
     nblocks = slot.shape[0]
     nrad = w_rad.shape[1]
@@ -86,6 +102,28 @@
     for device in greeted:
         pl.semaphore_signal(barrier, inc=1, device_id=device, device_id_type=MESH)
     pl.semaphore_signal(barrier, inc=1, device_id=sibling, device_id_type=MESH)
+    sources = (
+        feats_in,
+        pos_in,
+        spec_in,
+        gain_in,
+        probe_in,
+        slot_in,
+        count_in,
+        w_rad_in,
+        w_one_in,
+        w_two_in,
+        target_in,
+    )
+    places = (feats, pos, spec, gain, probe, slot, count, w_rad, w_one, w_two, target)
+    loads = [
+        pltpu.make_async_copy(source, place, load_sem.at[i])
+        for i, (source, place) in enumerate(zip(sources, places))
+    ]
+    for copy in loads:
+        copy.start()
+    for copy in loads:
+        copy.wait()
 
     nspec = gain.shape[0]
     onehot = (lax.broadcasted_iota(jnp.int32, (nspec, natoms), 0) == spec[...]).astype(jnp.float32)
@@ -159,13 +197,18 @@
     second = [(xi, yi) for xi, yi in remote if xi != 0 and yi != 0]
     for xi, yi in remote:
         pos_copy(xi, yi).start()
-    chunk_ids = range(len(CHUNKS))
-    for c in chunk_ids:
+    def start_y(c):
+        for xi, yi in along_y:
+            ici(c, xi, yi).start()
+
+    for c in X_ORDER:
         for xi, yi in along_x:
             ici(c, xi, yi).start()
-    for c in sorted(chunk_ids, key=lambda c: c not in Y_FIRST):
-        for xi, yi in along_y:
-            ici(c, xi, yi).start()
+        if c == 0:
+            start_y(0)
+        elif c == 1:
+            start_y(1)
+            start_y(3)
 
     def pass_x(c):
         for xi, yi in along_x:
@@ -244,58 +287,74 @@
         lax.fori_loop(0, PBLK // ROWS, strip, 0)
         return 0
 
-    def matmul(c):
-        low, high = CHUNKS[c]
-        for xi, yi in remote:
-            sib(c, xi, yi).wait_recv()
-
-        def one_block(block, _):
-            weights = []
+    def matmul(*group):
+        for c in group:
+            for xi, yi in remote:
+                sib(c, xi, yi).wait_recv()
+        for block in range(nblocks):
             cols = [column_of(block, entry) for entry in range(nentry)]
-            for k in range(high - low):
-                for entry in range(nentry):
-                    weights.append(tabs[c][cols[entry], k])
-            weights = jnp.concatenate(weights, axis=0)
+            weights = jnp.concatenate(
+                [
+                    tabs[c][cols[entry], k - CHUNKS[c][0]]
+                    for c in group
+                    for k in range(*CHUNKS[c])
+                    for entry in range(nentry)
+                ],
+                axis=0,
+            )
             lhs = jnp.concatenate(
                 [
                     edges[block, k, entry]
-                    for k in range(low, high)
+                    for c in group
+                    for k in range(*CHUNKS[c])
                     for entry in range(nentry)
                 ],
                 axis=1,
             )
             part = jnp.dot(lhs, weights, preferred_element_type=jnp.float32)
+            degree = DEGREE[group[0]]
             total = msg[block]
             for b in range(nrad):
-                total = total + part[b * PBLK : (b + 1) * PBLK] * w_rad[DEGREE[c], b : b + 1, :]
+                total = total + part[b * PBLK : (b + 1) * PBLK] * w_rad[degree, b : b + 1, :]
             msg[block] = total
-            return 0
-
-        lax.fori_loop(0, nblocks, one_block, 0)
 
     for xi, yi in remote:
         pos_copy(xi, yi).wait_recv()
     units = nblocks * nentry
-    lax.fori_loop(0, units // 8, edge_unit, 0)
+
+    def edge_part(low, high):
+        lax.fori_loop(low * units // 8, high * units // 8, edge_unit, 0)
+
+    edge_part(0, 1)
+    pass_y(0)
+    pass_x(0)
+    start_y(2)
+    edge_part(1, 4)
+    pass_y(1)
+    pass_y(3)
+    edge_part(4, 5)
+    pass_x(1)
+    start_y(4)
+    edge_part(5, 8)
+    pass_second(0)
     pass_y(2)
-    pass_y(3)
-    lax.fori_loop(units // 8, 4 * units // 8, edge_unit, 0)
-    pass_x(0)
-    pass_y(0)
-    lax.fori_loop(4 * units // 8, 6 * units // 8, edge_unit, 0)
-    pass_y(1)
-    lax.fori_loop(6 * units // 8, units, edge_unit, 0)
-    pass_x(1)
-    pass_second(0)
     pass_x(2)
-    matmul(0)
+    start_y(5)
+    pass_x(4)
+    pass_second(1)
+    pass_x(5)
+    matmul(0, 1)
+    pass_y(4)
+    pass_second(2)
     pass_x(3)
-    pass_second(1)
-    pass_second(2)
-    matmul(1)
+    pass_y(5)
+    matmul(2)
+    pass_second(4)
     pass_second(3)
-    matmul(2)
+    matmul(4)
+    pass_second(5)
     matmul(3)
+    matmul(5)
 
     message_bf = msg[...].reshape(nblocks * PBLK, chans).astype(jnp.bfloat16)
     pre = jnp.dot(message_bf, w_one[...], preferred_element_type=jnp.float32)
@@ -331,6 +390,7 @@
             shares_in,
             two_in,
             gathered,
+            two_total,
             pair_send,
             pair_recv,
             share_send,
@@ -340,9 +400,11 @@
             full_send,
             full_recv,
         ) = reduce_refs
-        upper = chans // 2
-        span = upper // chips
-        part[...] = local_one.reshape(2, upper, chans)
+        owners, span = gathered.shape[0], gathered.shape[1]
+        first = (chips - owners) // 2
+        mine = me - first
+        owning = jnp.logical_and(mine >= 0, mine < owners)
+        part[...] = local_one
         two_part[...] = local_two
 
         def to_sibling(index, source, dest):
@@ -355,57 +417,109 @@
                 device_id_type=MESH,
             )
 
-        def to_peer(offset, source, dest, send, recv):
+        def to_chip(chip, source, dest, send, recv):
             return pltpu.make_async_remote_copy(
                 src_ref=source,
                 dst_ref=dest,
-                send_sem=send.at[offset],
-                recv_sem=recv.at[offset],
-                device_id=peer(offset),
+                send_sem=send,
+                recv_sem=recv,
+                device_id={"gx": chip // ny, "gy": lax.rem(chip, ny)},
                 device_id_type=MESH,
             )
 
-        swaps = [to_sibling(0, part.at[1 - gz], pair_in), to_sibling(1, two_part, two_pair_in)]
-        for copy in swaps:
-            copy.start()
-        for copy in swaps:
-            copy.wait_recv()
-        chip_sum = part[gz] + pair_in[...]
-        shares[...] = chip_sum.reshape(chips, span, chans).astype(jnp.bfloat16)
-        two_sum = two_part[...] + two_pair_in[...]
-        two_share[...] = two_sum
-        two_in[me] = two_sum
-        scattered = []
-        for offset in offsets:
-            target_chip = lax.rem(me + offset, chips)
-            scattered.append(
-                to_peer(offset, shares.at[target_chip], shares_in.at[offset], share_send, share_recv)
+        def share_copy(w, source_chip):
+            return to_chip(
+                first + w,
+                shares.at[w],
+                shares_in.at[source_chip],
+                share_send.at[w],
+                share_recv.at[source_chip],
             )
-        twos = [to_peer(offset, two_share, two_in.at[me], two_send, two_recv) for offset in offsets]
-        for copy in scattered + twos:
-            copy.start()
-        total = shares[me].astype(jnp.float32)
-        for offset, copy in zip(offsets, scattered):
-            copy.wait_recv()
-            total = total + shares_in[offset].astype(jnp.float32)
-        gathered[gz, me] = total.astype(jnp.bfloat16)
-        spread = [
-            to_peer(offset, gathered.at[gz, me], gathered.at[gz, me], full_send, full_recv)
-            for offset in offsets
-        ]
-        for copy in spread:
-            copy.start()
-        for copy in twos:
-            copy.wait_recv()
-        two_out[...] = jnp.sum(two_in[...], axis=0)
-        for copy in spread:
-            copy.wait_recv()
-        swap_back = to_sibling(2, gathered.at[gz], gathered.at[gz])
-        swap_back.start()
-        swap_back.wait_recv()
+
+        def full_copy(chip, w):
+            return to_chip(chip, gathered.at[w], gathered.at[w], full_send.at[chip], full_recv.at[w])
+
+        def two_copy(chip, source_chip):
+            return to_chip(
+                chip, two_share, two_in.at[source_chip], two_send.at[chip], two_recv.at[source_chip]
+            )
+
+        def piece(w):
+            return to_sibling(3 + w, gathered.at[w], gathered.at[w])
+
+        swaps = [to_sibling(0, part, pair_in), to_sibling(1, two_part, two_pair_in)]
+        two_back = to_sibling(2, two_total, two_total)
+        others = [lax.rem(me + offset, chips) for offset in offsets]
+
+        @pl.when(gz == 0)
+        def _():
+            for copy in swaps:
+                copy.start()
+            two_back.wait_recv()
+            for w in range(owners):
+                piece(w).wait_recv()
+            for copy in swaps:
+                copy.wait_send()
+
+        @pl.when(gz == 1)
+        def _():
+            for copy in swaps:
+                copy.wait_recv()
+            chip_sum = part[...] + pair_in[...]
+            shares[...] = chip_sum.reshape(owners, span, chans).astype(jnp.bfloat16)
+            two_sum = two_part[...] + two_pair_in[...]
+            two_share[...] = two_sum
+            two_in[me] = two_sum
+            for w in range(owners):
+
+                @pl.when(mine != w)
+                def _(w=w):
+                    share_copy(w, me).start()
+
+            for chip in others:
+                two_copy(chip, me).start()
+
+            @pl.when(owning)
+            def _():
+                total = shares[mine].astype(jnp.float32)
+                for chip in others:
+                    share_copy(mine, chip).wait_recv()
+                    total = total + shares_in[chip].astype(jnp.float32)
+                gathered[mine] = total.astype(jnp.bfloat16)
+                for chip in others:
+                    full_copy(chip, mine).start()
+                piece(mine).start()
+
+            for chip in others:
+                two_copy(chip, chip).wait_recv()
+            two_total[...] = jnp.sum(two_in[...], axis=0)
+            two_back.start()
+            for w in range(owners):
+
+                @pl.when(mine != w)
+                def _(w=w):
+                    full_copy(me, w).wait_recv()
+                    piece(w).start()
+
+            for w in range(owners):
+
+                @pl.when(mine != w)
+                def _(w=w):
+                    share_copy(w, me).wait_send()
+
+                piece(w).wait_send()
+
+            @pl.when(owning)
+            def _():
+                for chip in others:
+                    full_copy(chip, mine).wait_send()
+
+            for chip in others:
+                two_copy(chip, me).wait_send()
+            two_back.wait_send()
+
         one_out[...] = gathered[...].reshape(chans, chans)
-        for copy in swaps + scattered + twos + spread + [swap_back]:
-            copy.wait_send()
+        two_out[...] = two_total[...]
 
     for xi, yi in remote:
         pos_copy(xi, yi).wait_send()
@@ -436,27 +550,42 @@
     nrad = w_rad.shape[1]
     ncol = 6 if ny == 2 else 9
     vmem = pl.BlockSpec(memory_space=pltpu.VMEM)
-    smem = pl.BlockSpec(memory_space=pltpu.SMEM)
     nchunk = len(CHUNKS)
     chips = nx * ny
-    fused = (chans // 2) % (16 * chips) == 0
+    owners = (nx // 2 if nx % 4 == 0 else nx) * ny
+    fused = chips <= FUSED_CHIPS and chans % (16 * owners) == 0
     reduce_scratch = []
     if fused:
-        span = chans // 2 // chips
+        span = chans // owners
         reduce_scratch = [
-            pltpu.VMEM((2, chans // 2, chans), jnp.float32),
+            pltpu.VMEM((chans, chans), jnp.float32),
             pltpu.VMEM((1, chans), jnp.float32),
-            pltpu.VMEM((chans // 2, chans), jnp.float32),
+            pltpu.VMEM((chans, chans), jnp.float32),
             pltpu.VMEM((1, chans), jnp.float32),
-            pltpu.VMEM((chips, span, chans), jnp.bfloat16),
+            pltpu.VMEM((owners, span, chans), jnp.bfloat16),
             pltpu.VMEM((1, chans), jnp.float32),
             pltpu.VMEM((chips, span, chans), jnp.bfloat16),
             pltpu.VMEM((chips, 1, chans), jnp.float32),
-            pltpu.VMEM((2, chips, span, chans), jnp.bfloat16),
-            pltpu.SemaphoreType.DMA((3,)),
-            pltpu.SemaphoreType.DMA((3,)),
+            pltpu.VMEM((owners, span, chans), jnp.bfloat16),
+            pltpu.VMEM((1, chans), jnp.float32),
+            pltpu.SemaphoreType.DMA((3 + owners,)),
+            pltpu.SemaphoreType.DMA((3 + owners,)),
             *[pltpu.SemaphoreType.DMA((chips,)) for _ in range(6)],
         ]
+    operands = (
+        atom_feats.reshape(natoms, -1),
+        atom_pos.reshape(3, 1, natoms),
+        species.reshape(1, natoms),
+        species_gain,
+        probe_pos,
+        pair_slot,
+        pair_count,
+        w_rad,
+        w_one,
+        w_two.reshape(1, chans),
+        target.reshape(nblocks, PBLK),
+    )
+    scalars = (5, 6)
     density, one, two = pl.pallas_call(
         functools.partial(kernel, nx, ny),
         out_shape=(
@@ -464,9 +593,14 @@
             jax.ShapeDtypeStruct((chans, chans), jnp.bfloat16 if fused else jnp.float32),
             jax.ShapeDtypeStruct((1, chans), jnp.float32),
         ),
-        in_specs=[vmem, vmem, vmem, vmem, vmem, smem, smem, vmem, vmem, vmem, vmem],
+        in_specs=[pl.BlockSpec(memory_space=pl.ANY)] * len(operands),
         out_specs=(vmem, vmem, vmem),
         scratch_shapes=[
+            *[
+                (pltpu.SMEM if i in scalars else pltpu.VMEM)(operand.shape, operand.dtype)
+                for i, operand in enumerate(operands)
+            ],
+            pltpu.SemaphoreType.DMA((len(operands),)),
             *[
                 pltpu.VMEM((ncol, high - low, natoms, chans), jnp.bfloat16)
                 for low, high in CHUNKS
@@ -486,19 +620,7 @@
         compiler_params=pltpu.CompilerParams(
             collective_id=0, has_side_effects=True, vmem_limit_bytes=60 * 1024 * 1024
         ),
-    )(
-        atom_feats.reshape(natoms, -1),
-        atom_pos.reshape(3, 1, natoms),
-        species.reshape(1, natoms),
-        species_gain,
-        probe_pos,
-        pair_slot,
-        pair_count,
-        w_rad,
-        w_one,
-        w_two.reshape(1, chans),
-        target.reshape(nblocks, PBLK),
-    )
+    )(*operands)
     two = two.reshape(chans)
     if fused:
         one = one.astype(jnp.float32)

time: 46.3 us -> 44.7 us (0.965)
  Pallas kernels: 42.6 us -> 41 us
    pallas_call x1, Pallas kernels: 42.6 us -> 41 us  [on_device(): pl.pallas_call(functools.partial(kernel, nx, ny), out_shape=(jax.ShapeDty...]
where the time goes in v1:
time: 44.7 us; the launch traced here: 44.5 us
  Pallas kernels  41 us (92%)
  other arithmetic  1.63 us (4%)
  local copies, waits for them, and re-layouts  1.23 us (3%)
  between operations  0.65 us (1%)
    pallas_call x1, Pallas kernels, on_device(): pl.pallas_call(functools.partial(kernel, nx, ny), out_shape=(jax.ShapeDty...  41 us
    convert_element_type x1, other arithmetic, on_device(): one = one.astype(jnp.float32)  1.63 us
    unnamed x6, local copies, waits for them, and re-layouts  1.23 us

profile of v1, /device:TPU:0, one launch (start us, length us, event | category | flops | bytes accessed | tf_op | source)
XLA Modules:
  0.0 44.5 jit_solution(11572859792748639790)
XLA Ops:
  0.6 41.0 %shard_map.130 = (f32[2,128]{1,0:T(2,128)}, bf16[256,256]{1,0:T(8,128)(2,1)}, f32[1,256]{1,0:T(1,128)}) custom-call(bf16[128,2304]{1,0:T(8,128)(2,1)} %bitcast.7, f32[3,1,128]{2,1,0:T(1,128)} %bitcast.8, s32[1,128]{1,0:T(1,128)} %bitcast.13, f32[5,256]{1,0:T(8,128)} %gain_in.1, f32[3,256]{1,0:T(4,128)} %probe_in.1, s32[2,4]{1,0:T(2,128)} %slot_in.1, ...), custom_call_target="tpu_custom_call" | custom-call | tf_op jit(solution)/shard_map/pallas_call | solution.py:589
  41.6 0.0 copy-start.1
  41.6 1.6 %convert_element_type.3 = f32[256,256]{1,0:T(8,128)} convert(bf16[256,256]{1,0:T(8,128)(2,1)} %get-tuple-element.7) | non-fusion elementwise | flops 65536 | bytes 393216 | tf_op jit(solution)/shard_map/convert_element_type | solution.py:626
  43.3 0.0 copy-done.1
  43.3 0.0 copy-start
  43.3 0.6 %copy.16 = f32[256]{0:T(256)} copy(f32[256]{0:T(256)S(1)} %bitcast.12) | data formatting | bytes 2048
  43.8 0.1 copy-done
  43.9 0.6 %copy.17 = f32[256]{0:T(256)} copy(f32[256]{0:T(256)S(1)} %bitcast.11) | data formatting | bytes 2048
Async XLA Ops:
  41.6 1.6 %copy-start.1 = (f32[2,128]{1,0:T(2,128)S(1)}, f32[2,128]{1,0:T(2,128)}, u32[]{:S(2)}) copy-start(f32[2,128]{1,0:T(2,128)} %get-tuple-element.6) | copy-start | bytes 3076
  43.3 0.7 %copy-start = (f32[1,256]{1,0:T(1,128)S(1)}, f32[1,256]{1,0:T(1,128)}, u32[]{:S(2)}) copy-start(f32[1,256]{1,0:T(1,128)} %get-tuple-element.8) | copy-start | bytes 3076

commit v2 on v1

--- a/solution.py
+++ b/solution.py
@@ -18,7 +18,6 @@
 CHUNKS = ((1, 2), (2, 4), (4, 6), (6, 8), (8, 9), (0, 1))
 DEGREE = (1, 1, 2, 2, 2, 0)
 Y_FIRST = (3,)
-X_ORDER = (0, 1, 2, 4, 5, 3)
 FUSED_CHIPS = 8
 ROWS = 16
 
@@ -201,14 +200,15 @@
         for xi, yi in along_y:
             ici(c, xi, yi).start()
 
-    for c in X_ORDER:
+    def start_x(c):
         for xi, yi in along_x:
             ici(c, xi, yi).start()
-        if c == 0:
-            start_y(0)
-        elif c == 1:
-            start_y(1)
-            start_y(3)
+
+    start_y(3)
+    for c in (0, 1, 2, 4, 5):
+        start_x(c)
+        start_y(c)
+    start_x(3)
 
     def pass_x(c):
         for xi, yi in along_x:
@@ -326,28 +326,24 @@
         lax.fori_loop(low * units // 8, high * units // 8, edge_unit, 0)
 
     edge_part(0, 1)
+    pass_y(3)
     pass_y(0)
     pass_x(0)
-    start_y(2)
-    edge_part(1, 4)
+    edge_part(1, 5)
     pass_y(1)
-    pass_y(3)
-    edge_part(4, 5)
     pass_x(1)
-    start_y(4)
     edge_part(5, 8)
-    pass_second(0)
     pass_y(2)
     pass_x(2)
-    start_y(5)
+    pass_second(0)
     pass_x(4)
     pass_second(1)
     pass_x(5)
     matmul(0, 1)
     pass_y(4)
+    pass_y(5)
     pass_second(2)
     pass_x(3)
-    pass_y(5)
     matmul(2)
     pass_second(4)
     pass_second(3)
@@ -589,9 +585,9 @@
     density, one, two = pl.pallas_call(
         functools.partial(kernel, nx, ny),
         out_shape=(
-            jax.ShapeDtypeStruct((nblocks, PBLK), jnp.float32),
-            jax.ShapeDtypeStruct((chans, chans), jnp.bfloat16 if fused else jnp.float32),
-            jax.ShapeDtypeStruct((1, chans), jnp.float32),
+            pltpu.VMEM((nblocks, PBLK), jnp.float32),
+            pltpu.VMEM((chans, chans), jnp.bfloat16 if fused else jnp.float32),
+            pltpu.VMEM((1, chans), jnp.float32),
         ),
         in_specs=[pl.BlockSpec(memory_space=pl.ANY)] * len(operands),
         out_specs=(vmem, vmem, vmem),

time: 44.7 us -> 42.7 us (0.955)
  other arithmetic: 1.63 us -> 0.72 us
  Pallas kernels: 41 us -> 40.1 us
    convert_element_type x1, other arithmetic: 1.63 us -> 0.72 us  [on_device(): one = one.astype(jnp.float32)]
    pallas_call x1, Pallas kernels: 41 us -> 40.1 us  [on_device(): pl.pallas_call(functools.partial(kernel, nx, ny), out_shape=(pltpu.VMEM((...]
    unnamed x6 -> x2, local copies, waits for them, and re-layouts: 1.23 us -> 1.13 us
where the time goes in v2:
time: 42.7 us; the launch traced here: 42.6 us
  Pallas kernels  40.1 us (94%)
  local copies, waits for them, and re-layouts  1.13 us (3%)
  other arithmetic  0.72 us (2%)
  between operations  0.64 us (1%)
    pallas_call x1, Pallas kernels, on_device(): pl.pallas_call(functools.partial(kernel, nx, ny), out_shape=(pltpu.VMEM((...  40.1 us
    unnamed x2, local copies, waits for them, and re-layouts  1.13 us

profile of v2, /device:TPU:0, one launch (start us, length us, event | category | flops | bytes accessed | tf_op | source)
XLA Modules:
  0.0 42.6 jit_solution(16875822525695031179)
XLA Ops:
  0.6 40.1 %shard_map.130 = (f32[2,128]{1,0:T(2,128)S(1)}, bf16[256,256]{1,0:T(8,128)(2,1)S(1)}, f32[1,256]{1,0:T(1,128)S(1)}) custom-call(bf16[128,2304]{1,0:T(8,128)(2,1)} %bitcast.9, f32[3,1,128]{2,1,0:T(1,128)} %bitcast.10, s32[1,128]{1,0:T(1,128)} %bitcast.13, f32[5,256]{1,0:T(8,128)} %gain_in.1, f32[3,256]{1,0:T(4,128)} %probe_in.1, s32[2,4]{1,0:T(2,128)} %slot_in.1, ...), custom_call_target="tpu_custom_call" | custom-call | tf_op jit(solution)/shard_map/pallas_call | solution.py:585
  40.7 0.6 %copy.16 = f32[256]{0:T(256)} copy(f32[256]{0:T(256)S(1)} %bitcast.8) | data formatting | bytes 2048
  41.3 0.6 %copy.17 = f32[256]{0:T(256)} copy(f32[256]{0:T(256)S(1)} %bitcast.7) | data formatting | bytes 2048
  41.9 0.7 %convert_element_type.3 = f32[256,256]{1,0:T(8,128)} convert(bf16[256,256]{1,0:T(8,128)(2,1)S(1)} %get-tuple-element.7) | non-fusion elementwise | flops 65536 | bytes 393216 | tf_op jit(solution)/shard_map/convert_element_type | solution.py:622
